TPU v7x, 256 devices: a whole 4x4x8 slice. The times are simulated.
256 devices in a mesh: ctx: 128 (over x, z, y_lo, core), head: 2 (over y_hi).
Axes of the slice: x: 4, y: 4 (y_hi: 2, y_lo: 2; y = y_hi * 2 + y_lo), z: 8, core: 2. Of those that a mesh axis runs over, the one named last changes fastest.
Arguments:
- queries: bfloat16 [32768, 512], P('ctx', 'head'), parts along dimension 1, may hold values from -32 to 32
- keys: bfloat16 [32768, 256], P('ctx', 'head'), parts along dimension 1, may hold values from -16 to 16
- values: bfloat16 [32768, 256], P('ctx', 'head'), parts along dimension 1, may hold values from -6 to 6
- doc_starts: int32 [6], P('head'), parts along dimension 0, may hold values from 1 to 12288, as said below
Outputs:
- attended: bfloat16 [32768, 512], P('ctx', 'head'), parts along dimension 1
There are 2 independent parts, one for each index of `head`. A program takes and returns all parts, laid end to end along the dimension named above; each array names one. Nothing has to cross between parts.
Inputs may be any that keep to these rules, and one draw needn't show every extreme that they name: `doc_starts`: strictly rising; the fourth document starts at exactly 12288.
All inputs are finite; a program needn't handle non-finite values.
Results may differ from a plain program's by a relative error of at most 0.01.
Values may be sent and summed in bfloat16 or wider, within the bound.
A program may use at most 64 MiB of HBM per device.

v0:
```python
import math
import jax
import jax.numpy as jnp
from jax import lax
from jax.sharding import PartitionSpec as P

D_HEAD = 128
Q_HEADS = 2
SCALE = 144.0 ** (-0.5)
NEGATIVE = -1e30


def doc_index(positions, doc_starts):
    return jnp.sum((positions[:, None] >= doc_starts[None, :]).astype(jnp.int32), axis=1)


def update_part(partial_value, target, key_block, block_start, doc_starts):
    query_rows, query_pos, query_doc, low_edge, high_edge = target
    key_count = key_block.shape[1]

    def attend(carried):
        row_max, row_total, weighted = carried
        key_pos = block_start + lax.iota(jnp.int32, key_count)
        key_doc = doc_index(key_pos, doc_starts)
        scores = (
            jnp.einsum("qhd,kd->hqk", query_rows, key_block[0], preferred_element_type=jnp.float32)
            * SCALE
        )
        visible = (key_pos[None, :] <= query_pos[:, None]) & (key_pos[None, :] >= low_edge)
        visible = (
            visible & (key_pos[None, :] < high_edge) & (key_doc[None, :] == query_doc[:, None])
        )
        scores = jnp.where(visible[None], scores, NEGATIVE)
        new_max = jnp.maximum(row_max, jnp.max(scores, axis=2))
        expo = jnp.where(visible[None], jnp.exp(scores - new_max[:, :, None]), 0.0)
        rescale = jnp.exp(row_max - new_max)
        row_total = row_total * rescale + jnp.sum(expo, axis=2)
        product = jnp.einsum(
            "hqk,kd->qhd",
            expo.astype(jnp.bfloat16),
            key_block[1],
            preferred_element_type=jnp.float32,
        )
        weighted = weighted * jnp.transpose(rescale)[:, :, None] + product
        return (new_max, row_total, weighted)

    needed = (block_start < high_edge) & (block_start + key_count > low_edge)
    return lax.cond(needed, attend, lambda carried: carried, partial_value)


def shards(queries, keys, values, doc_starts):
    shard_rows = queries.shape[0]
    my_index = lax.axis_index("ctx")
    row_iota = lax.iota(jnp.int32, shard_rows)
    own_pos = my_index * shard_rows + row_iota
    own_rows = queries.reshape(shard_rows, Q_HEADS, D_HEAD)
    own_doc = doc_index(own_pos, doc_starts)
    key_values = jnp.stack([keys, values])
    fresh_partial = (
        jnp.full((Q_HEADS, shard_rows), NEGATIVE, jnp.float32),
        jnp.zeros((Q_HEADS, shard_rows), jnp.float32),
        jnp.zeros((shard_rows, Q_HEADS, D_HEAD), jnp.float32),
    )
    targets = ((own_rows, own_pos, own_doc, jnp.int32(0), (my_index + 1) * shard_rows),)
    partials = tuple((fresh_partial for target in targets))
    shard_keys = lax.all_gather(key_values, "ctx", axis=1, tiled=True)
    key_total = shard_keys.shape[1]
    block_len = shard_rows * math.gcd(key_total // shard_rows, 4)

    def block_step(block_number, running):
        key_block = lax.dynamic_slice_in_dim(shard_keys, block_number * block_len, block_len, 1)
        block_start = block_number * block_len
        return tuple(
            (
                update_part(partial_value, target, key_block, block_start, doc_starts)
                for partial_value, target in zip(running, targets)
            )
        )

    partials = lax.fori_loop(0, key_total // block_len, block_step, partials)
    result = partials[0]
    row_max, row_total, weighted = result
    attended = weighted / jnp.transpose(row_total)[:, :, None]
    return attended.reshape(shard_rows, Q_HEADS * D_HEAD).astype(jnp.bfloat16)


def solution(mesh):
    in_specs = (P("ctx", "head"), P("ctx", "head"), P("ctx", "head"), P("head"))
    out_specs = P("ctx", "head")
    return jax.shard_map(shards, mesh=mesh, in_specs=in_specs, out_specs=out_specs, check_vma=False)
```

profile of v0, /device:TPU:230, one launch (start us, length us, event | category | flops | bytes accessed | tf_op | source)
XLA Modules:
  0.0 432.7 jit_solution(961604463259147152)
XLA Ops:
  10.0 225.3 %all-gather.2.cloned.1.call-done = bf16[2,32768,128]{2,1,0:T(8,128)(2,1)} async-done(((bf16[2,256,128]{2,1,0:T(8,128)(2,1)}), bf16[2,32768,128]{2,1,0:T(8,128)(2,1)}) %all-gather.2.cloned.1.call-update) | async-done | bytes 16777232 | tf_op jit(solution)/shard_map/all_gather | solution.py:66
  235.3 189.7 %while.18 = (s32[]{:T(128)}, f32[2,256]{1,0:T(2,128)S(1)}, f32[2,256]{1,0:T(2,128)S(1)}, f32[256,2,128]{2,0,1:T(8,128)S(1)}, s32[]{:T(128)}, /*index=5*/s32[3]{0...) while((s32[]{:T(128)}, f32[2,256]{1,0:T(2,128)S(1)}, ...), condition=%wide.region_7.8_spmd.clone, body=%wide.region_1.7_spmd.clone.sunk | while | flops 276707072 | bytes 8582549 | solution.py:80
  241.3 5.9 %conditional.3 = ((f32[2,256]{1,0:T(2,128)S(1)}, f32[2,256]{1,0:T(2,128)S(1)}, f32[256,2,128]{2,0,1:T(8,128)S(1)})) conditional(s32[]{:T(128)} %convert_element_type.37, (f32[2,256]{1,0:T(2,128)S(1)}, f32[2,256]{1,0:T(2,128)S(1)}, f32[256,2,128]{2,0,1:T(8,128)S(1)}) %tuple.50, (s32[]{:T(128)}, s32[]{:T(128)}, s32[]{:T(128)}, s32[3]{0:T(128)}, ...), branch_computations={%region_2.0_spmd, %region_3.6_spmd} | conditional | flops 276707072 | bytes 8581238 | solution.py:48
  247.2 5.9 %conditional.3 = ((f32[2,256]{1,0:T(2,128)S(1)}, f32[2,256]{1,0:T(2,128)S(1)}, f32[256,2,128]{2,0,1:T(8,128)S(1)})) conditional(s32[]{:T(128)} %convert_element_type.37, (f32[2,256]{1,0:T(2,128)S(1)}, f32[2,256]{1,0:T(2,128)S(1)}, f32[256,2,128]{2,0,1:T(8,128)S(1)}) %tuple.50, (s32[]{:T(128)}, s32[]{:T(128)}, s32[]{:T(128)}, s32[3]{0:T(128)}, ...), branch_computations={%region_2.0_spmd, %region_3.6_spmd} | conditional | flops 276707072 | bytes 8581238 | solution.py:48
  253.1 5.9 %conditional.3 = ((f32[2,256]{1,0:T(2,128)S(1)}, f32[2,256]{1,0:T(2,128)S(1)}, f32[256,2,128]{2,0,1:T(8,128)S(1)})) conditional(s32[]{:T(128)} %convert_element_type.37, (f32[2,256]{1,0:T(2,128)S(1)}, f32[2,256]{1,0:T(2,128)S(1)}, f32[256,2,128]{2,0,1:T(8,128)S(1)}) %tuple.50, (s32[]{:T(128)}, s32[]{:T(128)}, s32[]{:T(128)}, s32[3]{0:T(128)}, ...), branch_computations={%region_2.0_spmd, %region_3.6_spmd} | conditional | flops 276707072 | bytes 8581238 | solution.py:48
  259.1 5.9 %conditional.3 = ((f32[2,256]{1,0:T(2,128)S(1)}, f32[2,256]{1,0:T(2,128)S(1)}, f32[256,2,128]{2,0,1:T(8,128)S(1)})) conditional(s32[]{:T(128)} %convert_element_type.37, (f32[2,256]{1,0:T(2,128)S(1)}, f32[2,256]{1,0:T(2,128)S(1)}, f32[256,2,128]{2,0,1:T(8,128)S(1)}) %tuple.50, (s32[]{:T(128)}, s32[]{:T(128)}, s32[]{:T(128)}, s32[3]{0:T(128)}, ...), branch_computations={%region_2.0_spmd, %region_3.6_spmd} | conditional | flops 276707072 | bytes 8581238 | solution.py:48
  265.0 5.9 %conditional.3 = ((f32[2,256]{1,0:T(2,128)S(1)}, f32[2,256]{1,0:T(2,128)S(1)}, f32[256,2,128]{2,0,1:T(8,128)S(1)})) conditional(s32[]{:T(128)} %convert_element_type.37, (f32[2,256]{1,0:T(2,128)S(1)}, f32[2,256]{1,0:T(2,128)S(1)}, f32[256,2,128]{2,0,1:T(8,128)S(1)}) %tuple.50, (s32[]{:T(128)}, s32[]{:T(128)}, s32[]{:T(128)}, s32[3]{0:T(128)}, ...), branch_computations={%region_2.0_spmd, %region_3.6_spmd} | conditional | flops 276707072 | bytes 8581238 | solution.py:48
  270.9 5.9 %conditional.3 = ((f32[2,256]{1,0:T(2,128)S(1)}, f32[2,256]{1,0:T(2,128)S(1)}, f32[256,2,128]{2,0,1:T(8,128)S(1)})) conditional(s32[]{:T(128)} %convert_element_type.37, (f32[2,256]{1,0:T(2,128)S(1)}, f32[2,256]{1,0:T(2,128)S(1)}, f32[256,2,128]{2,0,1:T(8,128)S(1)}) %tuple.50, (s32[]{:T(128)}, s32[]{:T(128)}, s32[]{:T(128)}, s32[3]{0:T(128)}, ...), branch_computations={%region_2.0_spmd, %region_3.6_spmd} | conditional | flops 276707072 | bytes 8581238 | solution.py:48
  276.8 5.9 %conditional.3 = ((f32[2,256]{1,0:T(2,128)S(1)}, f32[2,256]{1,0:T(2,128)S(1)}, f32[256,2,128]{2,0,1:T(8,128)S(1)})) conditional(s32[]{:T(128)} %convert_element_type.37, (f32[2,256]{1,0:T(2,128)S(1)}, f32[2,256]{1,0:T(2,128)S(1)}, f32[256,2,128]{2,0,1:T(8,128)S(1)}) %tuple.50, (s32[]{:T(128)}, s32[]{:T(128)}, s32[]{:T(128)}, s32[3]{0:T(128)}, ...), branch_computations={%region_2.0_spmd, %region_3.6_spmd} | conditional | flops 276707072 | bytes 8581238 | solution.py:48
  282.8 5.9 %conditional.3 = ((f32[2,256]{1,0:T(2,128)S(1)}, f32[2,256]{1,0:T(2,128)S(1)}, f32[256,2,128]{2,0,1:T(8,128)S(1)})) conditional(s32[]{:T(128)} %convert_element_type.37, (f32[2,256]{1,0:T(2,128)S(1)}, f32[2,256]{1,0:T(2,128)S(1)}, f32[256,2,128]{2,0,1:T(8,128)S(1)}) %tuple.50, (s32[]{:T(128)}, s32[]{:T(128)}, s32[]{:T(128)}, s32[3]{0:T(128)}, ...), branch_computations={%region_2.0_spmd, %region_3.6_spmd} | conditional | flops 276707072 | bytes 8581238 | solution.py:48
  288.7 5.9 %conditional.3 = ((f32[2,256]{1,0:T(2,128)S(1)}, f32[2,256]{1,0:T(2,128)S(1)}, f32[256,2,128]{2,0,1:T(8,128)S(1)})) conditional(s32[]{:T(128)} %convert_element_type.37, (f32[2,256]{1,0:T(2,128)S(1)}, f32[2,256]{1,0:T(2,128)S(1)}, f32[256,2,128]{2,0,1:T(8,128)S(1)}) %tuple.50, (s32[]{:T(128)}, s32[]{:T(128)}, s32[]{:T(128)}, s32[3]{0:T(128)}, ...), branch_computations={%region_2.0_spmd, %region_3.6_spmd} | conditional | flops 276707072 | bytes 8581238 | solution.py:48
  294.6 5.9 %conditional.3 = ((f32[2,256]{1,0:T(2,128)S(1)}, f32[2,256]{1,0:T(2,128)S(1)}, f32[256,2,128]{2,0,1:T(8,128)S(1)})) conditional(s32[]{:T(128)} %convert_element_type.37, (f32[2,256]{1,0:T(2,128)S(1)}, f32[2,256]{1,0:T(2,128)S(1)}, f32[256,2,128]{2,0,1:T(8,128)S(1)}) %tuple.50, (s32[]{:T(128)}, s32[]{:T(128)}, s32[]{:T(128)}, s32[3]{0:T(128)}, ...), branch_computations={%region_2.0_spmd, %region_3.6_spmd} | conditional | flops 276707072 | bytes 8581238 | solution.py:48
  300.6 5.9 %conditional.3 = ((f32[2,256]{1,0:T(2,128)S(1)}, f32[2,256]{1,0:T(2,128)S(1)}, f32[256,2,128]{2,0,1:T(8,128)S(1)})) conditional(s32[]{:T(128)} %convert_element_type.37, (f32[2,256]{1,0:T(2,128)S(1)}, f32[2,256]{1,0:T(2,128)S(1)}, f32[256,2,128]{2,0,1:T(8,128)S(1)}) %tuple.50, (s32[]{:T(128)}, s32[]{:T(128)}, s32[]{:T(128)}, s32[3]{0:T(128)}, ...), branch_computations={%region_2.0_spmd, %region_3.6_spmd} | conditional | flops 276707072 | bytes 8581238 | solution.py:48
  306.5 5.9 %conditional.3 = ((f32[2,256]{1,0:T(2,128)S(1)}, f32[2,256]{1,0:T(2,128)S(1)}, f32[256,2,128]{2,0,1:T(8,128)S(1)})) conditional(s32[]{:T(128)} %convert_element_type.37, (f32[2,256]{1,0:T(2,128)S(1)}, f32[2,256]{1,0:T(2,128)S(1)}, f32[256,2,128]{2,0,1:T(8,128)S(1)}) %tuple.50, (s32[]{:T(128)}, s32[]{:T(128)}, s32[]{:T(128)}, s32[3]{0:T(128)}, ...), branch_computations={%region_2.0_spmd, %region_3.6_spmd} | conditional | flops 276707072 | bytes 8581238 | solution.py:48
  312.4 5.9 %conditional.3 = ((f32[2,256]{1,0:T(2,128)S(1)}, f32[2,256]{1,0:T(2,128)S(1)}, f32[256,2,128]{2,0,1:T(8,128)S(1)})) conditional(s32[]{:T(128)} %convert_element_type.37, (f32[2,256]{1,0:T(2,128)S(1)}, f32[2,256]{1,0:T(2,128)S(1)}, f32[256,2,128]{2,0,1:T(8,128)S(1)}) %tuple.50, (s32[]{:T(128)}, s32[]{:T(128)}, s32[]{:T(128)}, s32[3]{0:T(128)}, ...), branch_computations={%region_2.0_spmd, %region_3.6_spmd} | conditional | flops 276707072 | bytes 8581238 | solution.py:48
  318.3 5.9 %conditional.3 = ((f32[2,256]{1,0:T(2,128)S(1)}, f32[2,256]{1,0:T(2,128)S(1)}, f32[256,2,128]{2,0,1:T(8,128)S(1)})) conditional(s32[]{:T(128)} %convert_element_type.37, (f32[2,256]{1,0:T(2,128)S(1)}, f32[2,256]{1,0:T(2,128)S(1)}, f32[256,2,128]{2,0,1:T(8,128)S(1)}) %tuple.50, (s32[]{:T(128)}, s32[]{:T(128)}, s32[]{:T(128)}, s32[3]{0:T(128)}, ...), branch_computations={%region_2.0_spmd, %region_3.6_spmd} | conditional | flops 276707072 | bytes 8581238 | solution.py:48
  324.3 5.9 %conditional.3 = ((f32[2,256]{1,0:T(2,128)S(1)}, f32[2,256]{1,0:T(2,128)S(1)}, f32[256,2,128]{2,0,1:T(8,128)S(1)})) conditional(s32[]{:T(128)} %convert_element_type.37, (f32[2,256]{1,0:T(2,128)S(1)}, f32[2,256]{1,0:T(2,128)S(1)}, f32[256,2,128]{2,0,1:T(8,128)S(1)}) %tuple.50, (s32[]{:T(128)}, s32[]{:T(128)}, s32[]{:T(128)}, s32[3]{0:T(128)}, ...), branch_computations={%region_2.0_spmd, %region_3.6_spmd} | conditional | flops 276707072 | bytes 8581238 | solution.py:48
  330.2 5.9 %conditional.3 = ((f32[2,256]{1,0:T(2,128)S(1)}, f32[2,256]{1,0:T(2,128)S(1)}, f32[256,2,128]{2,0,1:T(8,128)S(1)})) conditional(s32[]{:T(128)} %convert_element_type.37, (f32[2,256]{1,0:T(2,128)S(1)}, f32[2,256]{1,0:T(2,128)S(1)}, f32[256,2,128]{2,0,1:T(8,128)S(1)}) %tuple.50, (s32[]{:T(128)}, s32[]{:T(128)}, s32[]{:T(128)}, s32[3]{0:T(128)}, ...), branch_computations={%region_2.0_spmd, %region_3.6_spmd} | conditional | flops 276707072 | bytes 8581238 | solution.py:48
  336.1 5.9 %conditional.3 = ((f32[2,256]{1,0:T(2,128)S(1)}, f32[2,256]{1,0:T(2,128)S(1)}, f32[256,2,128]{2,0,1:T(8,128)S(1)})) conditional(s32[]{:T(128)} %convert_element_type.37, (f32[2,256]{1,0:T(2,128)S(1)}, f32[2,256]{1,0:T(2,128)S(1)}, f32[256,2,128]{2,0,1:T(8,128)S(1)}) %tuple.50, (s32[]{:T(128)}, s32[]{:T(128)}, s32[]{:T(128)}, s32[3]{0:T(128)}, ...), branch_computations={%region_2.0_spmd, %region_3.6_spmd} | conditional | flops 276707072 | bytes 8581238 | solution.py:48
  342.1 5.9 %conditional.3 = ((f32[2,256]{1,0:T(2,128)S(1)}, f32[2,256]{1,0:T(2,128)S(1)}, f32[256,2,128]{2,0,1:T(8,128)S(1)})) conditional(s32[]{:T(128)} %convert_element_type.37, (f32[2,256]{1,0:T(2,128)S(1)}, f32[2,256]{1,0:T(2,128)S(1)}, f32[256,2,128]{2,0,1:T(8,128)S(1)}) %tuple.50, (s32[]{:T(128)}, s32[]{:T(128)}, s32[]{:T(128)}, s32[3]{0:T(128)}, ...), branch_computations={%region_2.0_spmd, %region_3.6_spmd} | conditional | flops 276707072 | bytes 8581238 | solution.py:48
  348.0 5.9 %conditional.3 = ((f32[2,256]{1,0:T(2,128)S(1)}, f32[2,256]{1,0:T(2,128)S(1)}, f32[256,2,128]{2,0,1:T(8,128)S(1)})) conditional(s32[]{:T(128)} %convert_element_type.37, (f32[2,256]{1,0:T(2,128)S(1)}, f32[2,256]{1,0:T(2,128)S(1)}, f32[256,2,128]{2,0,1:T(8,128)S(1)}) %tuple.50, (s32[]{:T(128)}, s32[]{:T(128)}, s32[]{:T(128)}, s32[3]{0:T(128)}, ...), branch_computations={%region_2.0_spmd, %region_3.6_spmd} | conditional | flops 276707072 | bytes 8581238 | solution.py:48
  353.9 5.9 %conditional.3 = ((f32[2,256]{1,0:T(2,128)S(1)}, f32[2,256]{1,0:T(2,128)S(1)}, f32[256,2,128]{2,0,1:T(8,128)S(1)})) conditional(s32[]{:T(128)} %convert_element_type.37, (f32[2,256]{1,0:T(2,128)S(1)}, f32[2,256]{1,0:T(2,128)S(1)}, f32[256,2,128]{2,0,1:T(8,128)S(1)}) %tuple.50, (s32[]{:T(128)}, s32[]{:T(128)}, s32[]{:T(128)}, s32[3]{0:T(128)}, ...), branch_computations={%region_2.0_spmd, %region_3.6_spmd} | conditional | flops 276707072 | bytes 8581238 | solution.py:48
  359.8 5.9 %conditional.3 = ((f32[2,256]{1,0:T(2,128)S(1)}, f32[2,256]{1,0:T(2,128)S(1)}, f32[256,2,128]{2,0,1:T(8,128)S(1)})) conditional(s32[]{:T(128)} %convert_element_type.37, (f32[2,256]{1,0:T(2,128)S(1)}, f32[2,256]{1,0:T(2,128)S(1)}, f32[256,2,128]{2,0,1:T(8,128)S(1)}) %tuple.50, (s32[]{:T(128)}, s32[]{:T(128)}, s32[]{:T(128)}, s32[3]{0:T(128)}, ...), branch_computations={%region_2.0_spmd, %region_3.6_spmd} | conditional | flops 276707072 | bytes 8581238 | solution.py:48
  419.1 5.9 %conditional.3 = ((f32[2,256]{1,0:T(2,128)S(1)}, f32[2,256]{1,0:T(2,128)S(1)}, f32[256,2,128]{2,0,1:T(8,128)S(1)})) conditional(s32[]{:T(128)} %convert_element_type.37, (f32[2,256]{1,0:T(2,128)S(1)}, f32[2,256]{1,0:T(2,128)S(1)}, f32[256,2,128]{2,0,1:T(8,128)S(1)}) %tuple.50, (s32[]{:T(128)}, s32[]{:T(128)}, s32[]{:T(128)}, s32[3]{0:T(128)}, ...), branch_computations={%region_2.0_spmd, %region_3.6_spmd} | conditional | flops 276707072 | bytes 8581238 | solution.py:48
  (405 shorter events, 248.7 us)
Async XLA Ops:
  6.5 228.7 %all-gather.2.cloned.1.call-start = ((), (), s32[]{:S(2)}) async-start(), calls=%async_computation | async-start | bytes 16908288 | tf_op jit(solution)/shard_map/all_gather | solution.py:66
Sparse Core Ops, SparseCore 0:
  9.2 226.0 all-gather.1
where the time goes:
time: 435 us; the launch traced here: 433 us
  waiting for transfers between devices  225 us (52%)
  matrix products  104 us (24%)
  other arithmetic  84.4 us (19%)
  between operations  13.4 us (3%)
    all_gather x1, waiting for transfers between devices, shards(): shard_keys = lax.all_gather(key_values, 'ctx', axis=1, tiled=True)  225 us
    dot_general x32, matrix products, attend(): jnp.einsum('hqk,kd->qhd', expo.astype(jnp.bfloat16), key_block[1], prefer...  59 us
    dot_general x32, matrix products, attend(): jnp.einsum('qhd,kd->hqk', query_rows, key_block[0], preferred_element_typ...  45.2 us
    and x32, other arithmetic, attend(): visible & (key_pos[None, :] < high_edge)  38.2 us
    reduce_sum x33, other arithmetic, doc_index(): jnp.sum((positions[:, None] >= doc_starts[None, :]).astype(jnp.int32), ax...  24.4 us
    reduce_sum x32, other arithmetic, attend(): row_total = row_total * rescale + jnp.sum(expo, axis=2)  18.1 us
  transfers between devices with their start and end apart: 1, of which 1 were waited for; matrix products, arithmetic and copies ran while one was open for 0% of the time, Pallas kernels for 0%

commit v1 on v0

--- a/solution.py
+++ b/solution.py
@@ -8,6 +8,9 @@
 Q_HEADS = 2
 SCALE = 144.0 ** (-0.5)
 NEGATIVE = -1e30
+prepare_joints = lambda v0: jnp.concatenate(
+    lax.all_to_all(jnp.stack(lax.axis_size("ctx") * [v0], axis=0), "ctx", 0, 0), axis=1
+)
 
 
 def doc_index(positions, doc_starts):
@@ -63,7 +66,7 @@
     )
     targets = ((own_rows, own_pos, own_doc, jnp.int32(0), (my_index + 1) * shard_rows),)
     partials = tuple((fresh_partial for target in targets))
-    shard_keys = lax.all_gather(key_values, "ctx", axis=1, tiled=True)
+    shard_keys = prepare_joints(key_values)
     key_total = shard_keys.shape[1]
     block_len = shard_rows * math.gcd(key_total // shard_rows, 4)
 

time: 435 us -> 567 us (1.30)
  waiting for transfers between devices: 225 us -> 363 us
  other arithmetic: 84.4 us -> 62 us
  local copies, waits for them, and re-layouts: 1.31 us -> 20.8 us
  between operations: 13.4 us -> 0.08 us
  starting transfers between devices: 0.01 us -> 11.9 us
    all_to_all x0 -> x1, waiting for transfers between devices: none -> 363 us  [lax.all_to_all(jnp.stack(lax.axis_size('ctx') * [v0], axis=0), 'ctx', 0, 0)]
    all_gather x1 -> x0, waiting for transfers between devices: 225 us -> none  [shards(): shard_keys = lax.all_gather(key_values, 'ctx', axis=1, tiled=True)]
    reduce_sum x33, other arithmetic: 24.4 us -> 2.73 us  [doc_index(): jnp.sum((positions[:, None] >= doc_starts[None, :]).astype(jnp.int32), ax...]
    all_to_all x0 -> x1, local copies, waits for them, and re-layouts: none -> 14.1 us  [lax.all_to_all(jnp.stack(lax.axis_size('ctx') * [v0], axis=0), 'ctx', 0, 0)]
    all_to_all x0 -> x1, starting transfers between devices: none -> 11.9 us  [lax.all_to_all(jnp.stack(lax.axis_size('ctx') * [v0], axis=0), 'ctx', 0, 0)]
    another operation x0 -> x1, local copies, waits for them, and re-layouts: none -> 6.32 us  [jnp.stack(lax.axis_size('ctx') * [v0], axis=0)]
where the time goes in v1:
time: 567 us; the launch traced here: 565 us
  waiting for transfers between devices  363 us (64%)
  matrix products  103 us (18%)
  other arithmetic  62 us (11%)
  local copies, waits for them, and re-layouts  20.8 us (4%)
  starting transfers between devices  11.9 us (2%)
    all_to_all x1, waiting for transfers between devices, lax.all_to_all(jnp.stack(lax.axis_size('ctx') * [v0], axis=0), 'ctx', 0, 0)  363 us
    dot_general x32, matrix products, attend(): jnp.einsum('hqk,kd->qhd', expo.astype(jnp.bfloat16), key_block[1], prefer...  58.4 us
    dot_general x32, matrix products, attend(): jnp.einsum('qhd,kd->hqk', query_rows, key_block[0], preferred_element_typ...  45 us
    and x32, other arithmetic, attend(): visible & (key_pos[None, :] < high_edge)  38.2 us
    reduce_sum x32, other arithmetic, attend(): row_total = row_total * rescale + jnp.sum(expo, axis=2)  18.1 us
    all_to_all x1, local copies, waits for them, and re-layouts, lax.all_to_all(jnp.stack(lax.axis_size('ctx') * [v0], axis=0), 'ctx', 0, 0)  14.1 us
    all_to_all x1, starting transfers between devices, lax.all_to_all(jnp.stack(lax.axis_size('ctx') * [v0], axis=0), 'ctx', 0, 0)  11.9 us
  transfers between devices with their start and end apart: 1, of which 1 were waited for; matrix products, arithmetic and copies ran while one was open for 0% of the time, Pallas kernels for 0%

profile of v1, /device:TPU:230, one launch (start us, length us, event | category | flops | bytes accessed | tf_op | source)
XLA Modules:
  0.0 564.6 jit_solution(10574905336456455535)
XLA Ops:
  0.9 6.3 %stack.11 = bf16[128,2,256,128]{3,2,1,0:T(8,128)(2,1)} broadcast(bf16[2,256,128]{2,1,0:T(8,128)(2,1)S(1)} %pad_maximum_fusion), dimensions={1,2,3} | broadcast | bytes 16908288 | tf_op jit(solution)/shard_map/stack | solution.py:12
  7.2 11.9 %all-to-all-start = ((bf16[128,2,256,128]{3,2,1,0:T(8,128)(2,1)}), bf16[128,2,256,128]{3,2,1,0:T(8,128)(2,1)}, u32[]{:S(2)}, u32[]{:S(2)}) async-start(bf16[128,2,256,128]{3,2,1,0:T(8,128)(2,1)} %stack.11), calls=%async_computation | async-start | bytes 33554432 | tf_op jit(solution)/shard_map/all_to_all | solution.py:12
  19.5 362.5 %all-to-all-done = bf16[128,2,256,128]{3,2,1,0:T(8,128)(2,1)} async-done(((bf16[128,2,256,128]{3,2,1,0:T(8,128)(2,1)}), bf16[128,2,256,128]{3,2,1,0:T(8,128)(2,1)}, u32[]{:S(2)}, u32[]{:S(2)}) %all-to-all-start) | async-done | bytes 16777248 | tf_op jit(solution)/shard_map/all_to_all | solution.py:12
  382.0 14.1 %copy.21 = bf16[128,2,256,128]{3,2,0,1:T(8,128)(2,1)} copy(bf16[128,2,256,128]{3,2,1,0:T(8,128)(2,1)} %all-to-all-done) | data formatting | bytes 33554432 | tf_op jit(solution)/shard_map/all_to_all | solution.py:12
  396.1 167.8 %while.18 = (s32[]{:T(128)}, f32[2,256]{1,0:T(2,128)S(1)}, f32[2,256]{1,0:T(2,128)S(1)}, f32[256,2,128]{2,0,1:T(8,128)S(1)}, s32[]{:T(128)}, /*index=5*/s32[3]{0...) while((s32[]{:T(128)}, f32[2,256]{1,0:T(2,128)S(1)}, ...), condition=%wide.region_7.8_spmd.clone, body=%wide.region_1.7_spmd.clone.sunk | while | flops 276707072 | bytes 8582549 | solution.py:83
  396.1 5.2 conditional.3
  401.4 5.2 conditional.3
  406.6 5.2 conditional.3
  417.1 5.2 conditional.3
  422.3 5.2 conditional.3
  427.6 5.2 conditional.3
  438.1 5.2 conditional.3
  443.3 5.2 conditional.3
  448.5 5.2 conditional.3
  459.0 5.2 conditional.3
  469.5 5.2 conditional.3
  480.0 5.2 conditional.3
  490.5 5.2 conditional.3
  501.0 5.2 conditional.3
  511.5 5.2 conditional.3
  521.9 5.2 conditional.3
  532.4 5.2 conditional.3
  542.9 5.2 conditional.3
  553.4 5.2 conditional.3
  (410 shorter events, 233.4 us)
Async XLA Ops:
  7.2 11.9 %copy-start = (bf16[256,256]{1,0:T(8,128)(2,1)S(1)}, bf16[256,256]{1,0:T(8,128)(2,1)}, u32[]{:S(2)}) copy-start(bf16[256,256]{1,0:T(8,128)(2,1)} %param.8) | copy-start | bytes 393220
  7.2 12.2 %copy-start.1 = (s32[3]{0:T(128)S(1)}, s32[3]{0:T(128)}, u32[]{:S(2)}) copy-start(s32[3]{0:T(128)} %param.11) | copy-start | bytes 40
  7.2 374.8 %all-to-all-start = ((bf16[128,2,256,128]{3,2,1,0:T(8,128)(2,1)}), bf16[128,2,256,128]{3,2,1,0:T(8,128)(2,1)}, u32[]{:S(2)}, u32[]{:S(2)}) async-start(bf16[128,2,256,128]{3,2,1,0:T(8,128)(2,1)} %stack.11), calls=%async_computation | async-start | bytes 33554432 | tf_op jit(solution)/shard_map/all_to_all | solution.py:12
